TPU v7x, 32 devices: a whole 2x2x4 slice. The times are simulated.
32 devices in a mesh: col: 16 (over z, y, x), grp: 2 (over core).
Axes of the slice: x: 2, y: 2, z: 4, core: 2. Of those that a mesh axis runs over, the one named last changes fastest.
Arguments:
- diag_blocks: float32 [16, 128, 128], P('col'), as said below
- panel_blocks: float32 [16, 2, 128, 128], P('col', 'grp'), as said below
- targets: int32 [16, 2], replicated, may hold values from 0 to 16, as said below
Outputs:
- factor_diag: float32 [16, 128, 128], P('col')
- factor_panel: float32 [16, 2, 128, 128], P('col', 'grp')
Inputs may be any that keep to these rules, and one draw needn't show every extreme that they name: targets[s, 0] is the parent of supernode s and targets[s, 1] = targets[targets[s, 0], 0] its grandparent, 16 where that ancestor lies outside the window; the tree is a binary heap under a random labelling: exactly one root, every supernode has at most two children and at most four grandchildren, and level d holds min(2 ** d, 16 - 2 ** d + 1) supernodes. `diag_blocks`: each block is symmetric positive definite, and every updated diagonal block stays positive definite. `panel_blocks`: every entry lies within 8 / sqrt(128) of zero.
All inputs are finite; a program needn't handle non-finite values.
Results may differ from a plain program's by a relative error of at most 0.00095.
Values may be sent and summed in bfloat16 or wider, within the bound.
A program may use at most 64 MiB of HBM per device.

v0:
```python
import jax
import jax.numpy as jnp
from jax import lax
from jax.sharding import PartitionSpec as P


def spread(x, axis, root):
    mine = lax.axis_index(axis) == root
    return lax.psum(jnp.where(mine, x, jnp.zeros_like(x)), axis)


def from_partner(x, axis, apart):
    return lax.ppermute(x, axis, [(i, i ^ 1 << apart) for i in range(lax.axis_size(axis))])


def node_depth(parent, nodes):
    extended = jnp.concatenate([parent, jnp.array([nodes], jnp.int32)])
    depth = jnp.zeros((nodes,), jnp.int32)
    current = parent
    for index in range(nodes.bit_length()):
        depth = depth + (current < nodes).astype(jnp.int32)
        current = extended[current]
    return depth


def solve_right(lower, panel):

    def one(factor, block):
        return jax.scipy.linalg.solve_triangular(factor, block.T, lower=True).T

    return jax.vmap(one)(lower, panel)


def sibling_rank(target, nodes):
    earlier = jnp.arange(nodes)[None, :] < jnp.arange(nodes)[:, None]
    same = target[:, None] == target[None, :]
    return jnp.sum((same & earlier).astype(jnp.int32), axis=1)


def slot_picker(target, rank, active_nodes, owned_ids, count):
    match = target[None, None, :] == owned_ids[:, None, None]
    match = match & (rank[None, None, :] == jnp.arange(count)[None, :, None])
    match = match & active_nodes[None, None, :]
    return match.astype(jnp.bfloat16)


def select_rows(picker, block_list):
    return jnp.einsum("iqc,cab->iqab", picker, block_list, preferred_element_type=jnp.float32)


def outer_sum(block_list):
    return jnp.einsum("hync,hyxc->hnx", block_list, block_list, preferred_element_type=jnp.float32)


def cross_sum(left_factor, right_factor):
    return jnp.einsum(
        "hync,hyxc->hnx", left_factor, right_factor, preferred_element_type=jnp.float32
    )


def pair_cores(sent):
    return lax.all_gather(sent[:, None], "grp", axis=1, tiled=True)


def spread_nodes(sent, active_nodes, pick_near, pick_far, slots, nodes, present, blanks):
    paired = pair_cores(sent)
    order = jnp.argsort(jnp.where(active_nodes, 0, 1) * nodes + jnp.arange(nodes, dtype=jnp.int32))

    def visit(index, carry):
        node = order[index]
        piece = lax.dynamic_index_in_dim(paired, node % slots, 0, keepdims=False)
        arrived = spread(piece, "col", node // slots).astype(jnp.float32)
        weight_near = lax.dynamic_index_in_dim(pick_near, node, 2, keepdims=False).astype(
            jnp.float32
        )
        weight_far = lax.dynamic_index_in_dim(pick_far, node, 2, keepdims=False).astype(jnp.float32)
        return (
            carry[0] + weight_near[:, :, None, None] * arrived[0][None, None],
            carry[1] + weight_far[:, :, None, None] * arrived[1][None, None],
            carry[2] + weight_near[:, :, None, None] * arrived[1][None, None],
        )

    return lax.fori_loop(0, present, visit, blanks)


def shards(diag_blocks, panel_blocks, targets):
    slots = diag_blocks.shape[0]
    width = diag_blocks.shape[1]
    nodes = targets.shape[0]
    core = lax.axis_index("grp")
    owned_ids = lax.axis_index("col") * slots + jnp.arange(slots, dtype=jnp.int32)
    parent = targets[:, 0]
    grand = targets[:, 1]
    depth = node_depth(parent, nodes)
    rank_near = sibling_rank(parent, nodes)
    rank_far = sibling_rank(grand, nodes)
    owned_tree_depth = jnp.take(depth, owned_ids)
    acc_diag = diag_blocks
    acc_panel = panel_blocks[:, 0]
    out_diag = jnp.zeros_like(diag_blocks)
    output_panel = jnp.zeros_like(acc_panel)
    empty_pair_slots = jnp.zeros((slots, 2, width, width), jnp.float32)
    blank_four = jnp.zeros((slots, 4, width, width), jnp.float32)
    for level in range(nodes.bit_length() - 1, -1, -1):
        wide_mask = (owned_tree_depth == level)[:, None, None]
        lower = jnp.linalg.cholesky(acc_diag)
        solved = solve_right(lower, acc_panel)
        out_diag = jnp.where(wide_mask, lower, out_diag)
        output_panel = jnp.where(wide_mask, solved, output_panel)
        if level == 0:
            break
        sent = jnp.where(wide_mask, solved, 0.0).astype(jnp.bfloat16)
        active_nodes = depth == level
        pick_near = slot_picker(parent, rank_near, active_nodes, owned_ids, 2)
        pick_far = slot_picker(grand, rank_far, active_nodes, owned_ids, 4)
        present = min(2**level, nodes - 2**level + 1)
        crowded = present * 4 > nodes
        if crowded:
            piece = lax.all_gather(sent, "col", axis=0, tiled=True)
            near_rows = select_rows(pick_near, piece)
            far_rows = select_rows(pick_far, piece)
            near_rows = near_rows.astype(jnp.bfloat16)
            far_rows = far_rows.astype(jnp.bfloat16)
            own_update = lax.cond(
                core == 0, lambda: outer_sum(near_rows), lambda: outer_sum(far_rows)
            )
            other_update, other_rows = (
                from_partner(own_update.astype(jnp.bfloat16), "grp", 0).astype(own_update.dtype),
                from_partner(near_rows, "grp", 0),
            )
            schur_update = own_update + other_update
            cross = cross_sum(other_rows, near_rows)
        else:
            kids, grandkids, kids_far = spread_nodes(
                sent,
                active_nodes,
                pick_near,
                pick_far,
                slots,
                nodes,
                present,
                (empty_pair_slots, blank_four, empty_pair_slots),
            )
            kids = kids.astype(jnp.bfloat16)
            schur_update = outer_sum(kids) + outer_sum(grandkids.astype(jnp.bfloat16))
            cross = cross_sum(kids_far.astype(jnp.bfloat16), kids)
        acc_diag = acc_diag - schur_update
        acc_panel = acc_panel - jnp.where(core == 0, cross, 0.0)
    return (out_diag, output_panel[:, None])


def solution(mesh):
    placed = (P("col", None, None), P("col", "grp", None, None), P())
    return jax.shard_map(
        shards,
        mesh=mesh,
        in_specs=placed,
        out_specs=(P("col", None, None), P("col", "grp", None, None)),
        check_vma=False,
    )
```

profile of v0, /device:TPU:0, one launch (start us, length us, event | category | flops | bytes accessed | tf_op | source)
XLA Modules:
  0.0 962.0 jit_solution(17685611445959303273)
XLA Ops:
  7.2 0.6 copy-done.2
  7.9 0.7 gather_fusion
  8.6 0.7 gather_fusion.1
  9.3 0.7 gather_fusion.2
  10.0 0.7 gather_fusion.3
  10.7 0.7 dynamic-slice.2
  11.5 11.7 %custom-call.20 = f32[1,128,128]{2,1,0:T(8,128)S(1)} custom-call(f32[1,128,128]{2,1,0:T(8,128)S(1)} %fusion.50), custom_call_target="Cholesky" | custom-call | tf_op jit(solution)/shard_map/jit(cholesky)/cholesky | solution.py:106
  23.2 0.7 compare_reduce_fusion.4
  23.9 0.7 fusion.69
  24.5 9.8 %custom-call.21 = f32[1,1,128,128]{2,3,1,0:T(8,128)S(1)} custom-call(f32[1,1,128,128]{3,2,1,0:T(8,128)S(1)} %fusion.69), custom_call_target="InvertDiagBlocksLowerTriangular" | custom-call | tf_op jit(solution)/shard_map/vmap(jit(_solve_triangular))/triangular_solve | solution.py:29
  35.5 2.2 all-gather
  37.7 1.2 sort.45
  39.0 0.6 broadcast_select_fusion
  39.9 0.6 dynamic-slice.3
  40.6 0.7 fusion.114
  41.4 0.7 fusion.112
  42.0 103.8 %all-reduce.4.cloned.1.call-done = bf16[2,128,128]{2,1,0:T(8,128)(2,1)} async-done(((bf16[2,128,128]{2,1,0:T(8,128)(2,1)}), bf16[2,128,128]{2,1,0:T(8,128)(2,1)}) %all-reduce.4.cloned.1.call-update) | async-done | bytes 65552 | tf_op jit(solution)/shard_map/while/body/eval_jaxpr/psum | solution.py:9
  145.9 0.8 convert_element_type.377
  147.6 11.7 %custom-call.22 = f32[1,128,128]{2,1,0:T(8,128)S(1)} custom-call(f32[1,128,128]{2,1,0:T(8,128)S(1)} %fusion.48), custom_call_target="Cholesky" | custom-call | tf_op jit(solution)/shard_map/jit(cholesky)/cholesky | solution.py:106
  159.3 0.7 compare_reduce_fusion.3
  160.0 0.6 fusion.70
  160.7 9.8 %custom-call.23 = f32[1,1,128,128]{2,3,1,0:T(8,128)S(1)} custom-call(f32[1,1,128,128]{3,2,1,0:T(8,128)S(1)} %fusion.70), custom_call_target="InvertDiagBlocksLowerTriangular" | custom-call | tf_op jit(solution)/shard_map/vmap(jit(_solve_triangular))/triangular_solve | solution.py:29
  170.9 41.8 %all_gather.13 = bf16[16,128,128]{2,1,0:T(8,128)(2,1)S(1)} all-gather(bf16[1,128,128]{2,1,0:T(8,128)(2,1)S(1)} %copy.89), channel_id=1, replica_groups=mesh['col'=16,'grp'=2] {'col'}, dimensions={0}, use_global_device_ids=true | all-gather | bytes 557056 | tf_op jit(solution)/shard_map/all_gather | solution.py:119
  214.0 1.2 sort.46
  215.3 1.2 sort.47
  217.1 11.7 %custom-call.24 = f32[1,128,128]{2,1,0:T(8,128)S(1)} custom-call(f32[1,128,128]{2,1,0:T(8,128)S(1)} %fusion.45), custom_call_target="Cholesky" | custom-call | tf_op jit(solution)/shard_map/jit(cholesky)/cholesky | solution.py:106
  228.8 0.7 compare_reduce_fusion.2
  229.5 0.6 fusion.71
  230.1 9.8 %custom-call.25 = f32[1,1,128,128]{2,3,1,0:T(8,128)S(1)} custom-call(f32[1,1,128,128]{3,2,1,0:T(8,128)S(1)} %fusion.71), custom_call_target="InvertDiagBlocksLowerTriangular" | custom-call | tf_op jit(solution)/shard_map/vmap(jit(_solve_triangular))/triangular_solve | solution.py:29
  240.6 2.1 all-gather.1
  242.7 438.1 %while.48 = (s32[]{:T(128)}, f32[1,2,128,128]{3,2,1,0:T(8,128)S(1)}, f32[1,4,128,128]{3,2,1,0:T(8,128)S(1)}, f32[1,2,128,128]{3,2,1,0:T(8,128)S(1)}, s32[16]{0:T...) while((s32[]{:T(128)}, ...), condition=%wide.region_11.14_spmd.clone, body=%wide.region_9.13_spmd.clone.sunk | while | flops 491536 | bytes 2228556 | solution.py:83
  242.7 0.7 dynamic_slice.120
  244.0 0.6 select_bitcast_fusion.5
  246.6 102.4 %all-reduce.6.cloned.1.call-done = bf16[2,128,128]{2,1,0:T(8,128)(2,1)} async-done(((bf16[2,128,128]{2,1,0:T(8,128)(2,1)}), bf16[2,128,128]{2,1,0:T(8,128)(2,1)}) %all-reduce.6.cloned.1.call-update) | async-done | bytes 65552 | tf_op jit(solution)/shard_map/while/body/eval_jaxpr/psum | solution.py:9
  349.0 0.8 convert_element_type.518
  350.1 0.7 dynamic_slice.120
  351.4 0.6 select_bitcast_fusion.5
  354.0 105.5 %all-reduce.6.cloned.1.call-done = bf16[2,128,128]{2,1,0:T(8,128)(2,1)} async-done(((bf16[2,128,128]{2,1,0:T(8,128)(2,1)}), bf16[2,128,128]{2,1,0:T(8,128)(2,1)}) %all-reduce.6.cloned.1.call-update) | async-done | bytes 65552 | tf_op jit(solution)/shard_map/while/body/eval_jaxpr/psum | solution.py:9
  459.4 0.8 convert_element_type.518
  460.6 0.7 dynamic_slice.120
  461.8 0.6 select_bitcast_fusion.5
  464.4 105.2 %all-reduce.6.cloned.1.call-done = bf16[2,128,128]{2,1,0:T(8,128)(2,1)} async-done(((bf16[2,128,128]{2,1,0:T(8,128)(2,1)}), bf16[2,128,128]{2,1,0:T(8,128)(2,1)}) %all-reduce.6.cloned.1.call-update) | async-done | bytes 65552 | tf_op jit(solution)/shard_map/while/body/eval_jaxpr/psum | solution.py:9
  569.6 0.8 convert_element_type.518
  570.7 0.7 dynamic_slice.120
  572.0 0.6 select_bitcast_fusion.5
  574.5 105.2 %all-reduce.6.cloned.1.call-done = bf16[2,128,128]{2,1,0:T(8,128)(2,1)} async-done(((bf16[2,128,128]{2,1,0:T(8,128)(2,1)}), bf16[2,128,128]{2,1,0:T(8,128)(2,1)}) %all-reduce.6.cloned.1.call-update) | async-done | bytes 65552 | tf_op jit(solution)/shard_map/while/body/eval_jaxpr/psum | solution.py:9
  679.7 0.8 convert_element_type.518
  681.3 11.7 %custom-call.26 = f32[1,128,128]{2,1,0:T(8,128)S(1)} custom-call(f32[1,128,128]{2,1,0:T(8,128)S(1)} %fusion.41), custom_call_target="Cholesky" | custom-call | tf_op jit(solution)/shard_map/jit(cholesky)/cholesky | solution.py:106
  693.0 0.7 compare_reduce_fusion.1
  693.7 0.6 fusion.72
  694.4 9.8 %custom-call.27 = f32[1,1,128,128]{2,3,1,0:T(8,128)S(1)} custom-call(f32[1,1,128,128]{3,2,1,0:T(8,128)S(1)} %fusion.72), custom_call_target="InvertDiagBlocksLowerTriangular" | custom-call | tf_op jit(solution)/shard_map/vmap(jit(_solve_triangular))/triangular_solve | solution.py:29
  704.8 2.2 all-gather.2
  706.9 220.6 %while.49 = (s32[]{:T(128)}, f32[1,2,128,128]{3,2,1,0:T(8,128)S(1)}, f32[1,4,128,128]{3,2,1,0:T(8,128)S(1)}, f32[1,2,128,128]{3,2,1,0:T(8,128)S(1)}, s32[16]{0:T...) while((s32[]{:T(128)}, ...), condition=%wide.region_15.18_spmd.clone, body=%wide.region_13.17_spmd.clone.sunk | while | flops 491536 | bytes 2228556 | solution.py:83
  708.2 0.6 select_bitcast_fusion.6
  710.8 105.1 %all-reduce.8.cloned.1.call-done = bf16[2,128,128]{2,1,0:T(8,128)(2,1)} async-done(((bf16[2,128,128]{2,1,0:T(8,128)(2,1)}), bf16[2,128,128]{2,1,0:T(8,128)(2,1)}) %all-reduce.8.cloned.1.call-update) | async-done | bytes 65552 | tf_op jit(solution)/shard_map/while/body/eval_jaxpr/psum | solution.py:9
  816.0 0.8 convert_element_type.519
  818.4 0.6 select_bitcast_fusion.6
  821.0 105.4 %all-reduce.8.cloned.1.call-done = bf16[2,128,128]{2,1,0:T(8,128)(2,1)} async-done(((bf16[2,128,128]{2,1,0:T(8,128)(2,1)}), bf16[2,128,128]{2,1,0:T(8,128)(2,1)}) %all-reduce.8.cloned.1.call-update) | async-done | bytes 65552 | tf_op jit(solution)/shard_map/while/body/eval_jaxpr/psum | solution.py:9
  926.4 0.8 convert_element_type.519
  928.0 11.7 %custom-call.28 = f32[1,128,128]{2,1,0:T(8,128)S(1)} custom-call(f32[1,128,128]{2,1,0:T(8,128)S(1)} %fusion.36), custom_call_target="Cholesky" | custom-call | tf_op jit(solution)/shard_map/jit(cholesky)/cholesky | solution.py:106
  939.7 0.6 compare_reduce_fusion
  940.4 3.8 select_bitcast_fusion.2
  944.2 9.8 %custom-call.29 = f32[1,1,128,128]{2,3,1,0:T(8,128)S(1)} custom-call(f32[1,1,128,128]{3,2,1,0:T(8,128)S(1)} %get-tuple-element.605), custom_call_target="InvertDiagBlocksLowerTriangular" | custom-call | tf_op jit(solution)/shard_map/vmap(jit(_solve_triangular))/triangular_solve | solution.py:29
  954.5 0.7 copy.107
  (124 shorter events, 9.7 us)
Async XLA Ops:
  7.2 0.7 copy-start.2
  7.2 138.7 %all-reduce.4.cloned.1.call-start = ((), (), s32[]{:S(2)}) async-start(), calls=%async_computation | async-start | bytes 131072 | tf_op jit(solution)/shard_map/while/body/eval_jaxpr/psum | solution.py:9
  10.0 1.4 copy-start
  23.9 11.2 %copy-start.1 = (f32[1,1,128,128]{3,2,1,0:T(8,128)S(1)}, f32[1,1,128,128]{3,2,1,0:T(8,128)}, u32[]{:S(2)}) copy-start(f32[1,1,128,128]{3,2,1,0:T(8,128)} %param.14) | copy-start | bytes 196612
  213.9 3.1 collective-permute-start
  216.5 23.4 %collective-permute-start.1 = (bf16[1,2,128,128]{3,1,2,0:T(2,128)(2,1)S(1)}, bf16[1,2,128,128]{3,1,2,0:T(2,128)(2,1)S(1)}, u32[]{:S(2)}, u32[]{:S(2)}) collective-permute-start(bf16[1,2,128,128]{3,1,2,0:T(2,128)(2,1)S(1)} %bitcast.322), channel_id=1, source_target_pairs={{0,1},{1,0},{2,3},{3,2},{4,5},{5,4},{6,7},{7,6},{8,9},{9,8},{10,11... | collective-permute-start | bytes 196616 | tf_op jit(solution)/shard_map/ppermute | solution.py:13
  242.7 106.3 %all-reduce.6.cloned.1.call-start = ((), (), s32[]{:S(2)}) async-start(), calls=%async_computation.1 | async-start | bytes 131072 | tf_op jit(solution)/shard_map/while/body/eval_jaxpr/psum | solution.py:9
  350.0 109.4 %all-reduce.6.cloned.1.call-start = ((), (), s32[]{:S(2)}) async-start(), calls=%async_computation.1 | async-start | bytes 131072 | tf_op jit(solution)/shard_map/while/body/eval_jaxpr/psum | solution.py:9
  460.5 109.1 %all-reduce.6.cloned.1.call-start = ((), (), s32[]{:S(2)}) async-start(), calls=%async_computation.1 | async-start | bytes 131072 | tf_op jit(solution)/shard_map/while/body/eval_jaxpr/psum | solution.py:9
  570.6 109.1 %all-reduce.6.cloned.1.call-start = ((), (), s32[]{:S(2)}) async-start(), calls=%async_computation.1 | async-start | bytes 131072 | tf_op jit(solution)/shard_map/while/body/eval_jaxpr/psum | solution.py:9
  706.9 109.0 %all-reduce.8.cloned.1.call-start = ((), (), s32[]{:S(2)}) async-start(), calls=%async_computation.2 | async-start | bytes 131072 | tf_op jit(solution)/shard_map/while/body/eval_jaxpr/psum | solution.py:9
  817.1 109.4 %all-reduce.8.cloned.1.call-start = ((), (), s32[]{:S(2)}) async-start(), calls=%async_computation.2 | async-start | bytes 131072 | tf_op jit(solution)/shard_map/while/body/eval_jaxpr/psum | solution.py:9
Sparse Core Ops, SparseCore 0:
  39.7 106.0 all-reduce.3
  249.5 99.3 all-reduce.5
  356.9 102.4 all-reduce.5
  467.0 102.4 all-reduce.5
  577.2 102.4 all-reduce.5
  713.5 102.4 all-reduce.7
  823.9 102.4 all-reduce.7
where the time goes:
time: 963 us; the launch traced here: 962 us
  waiting for transfers between devices  733 us (76%)
  other arithmetic  135 us (14%)
  blocking collectives  48.3 us (5%)
  loops' own time  15.8 us (2%)
  between operations  15.4 us (2%)
  local copies, waits for them, and re-layouts  10 us (1%)
    psum x7, waiting for transfers between devices, spread(): return lax.psum(jnp.where(mine, x, jnp.zeros_like(x)), axis)  733 us
    another operation x15, other arithmetic, shards(): lower = jnp.linalg.cholesky(acc_diag)  62.1 us
    another operation x10, other arithmetic, one(): return jax.scipy.linalg.solve_triangular(factor, block.T, lower=True).T  55.4 us
    all_gather x1, blocking collectives, shards(): piece = lax.all_gather(sent, 'col', axis=0, tiled=True)  41.8 us
  transfers between devices with their start and end apart: 9, of which 7 were waited for; matrix products, arithmetic and copies ran while one was open for 3% of the time, Pallas kernels for 0%

commit v1 on v0

--- a/solution.py
+++ b/solution.py
@@ -2,11 +2,14 @@
 import jax.numpy as jnp
 from jax import lax
 from jax.sharding import PartitionSpec as P
+from jax.lax import all_gather
+
+open_the_skins = lambda z, along_axis: jnp.sum(all_gather(z, along_axis), 0)
 
 
 def spread(x, axis, root):
     mine = lax.axis_index(axis) == root
-    return lax.psum(jnp.where(mine, x, jnp.zeros_like(x)), axis)
+    return open_the_skins(jnp.where(mine, x, jnp.zeros_like(x)), axis)
 
 
 def from_partner(x, axis, apart):

time: 963 us -> 611 us (0.63)
  waiting for transfers between devices: 733 us -> 377 us
    psum x7 -> x0, waiting for transfers between devices: 733 us -> none  [spread(): return lax.psum(jnp.where(mine, x, jnp.zeros_like(x)), axis)]
    all_gather x0 -> x7, waiting for transfers between devices: none -> 377 us  [open_the_skins = lambda z, along_axis: jnp.sum(all_gather(z, along_axis), 0)]
  transfers between devices with their start and end apart: 9 -> 9, of which waited for: 7 -> 7; matrix products, arithmetic and copies ran while one was open for 3% -> 5% of each run, Pallas kernels for 0% -> 0%
where the time goes in v1:
time: 611 us; the launch traced here: 610 us
  waiting for transfers between devices  377 us (62%)
  other arithmetic  139 us (23%)
  blocking collectives  47.9 us (8%)
  loops' own time  15.8 us (3%)
  between operations  15.5 us (3%)
  local copies, waits for them, and re-layouts  10.3 us (2%)
    all_gather x7, waiting for transfers between devices, open_the_skins = lambda z, along_axis: jnp.sum(all_gather(z, along_axis), 0)  377 us
    another operation x15, other arithmetic, shards(): lower = jnp.linalg.cholesky(acc_diag)  62.1 us
    another operation x10, other arithmetic, one(): return jax.scipy.linalg.solve_triangular(factor, block.T, lower=True).T  55.3 us
    all_gather x1, blocking collectives, shards(): piece = lax.all_gather(sent, 'col', axis=0, tiled=True)  41.5 us
    another operation x2, loops' own time, spread_nodes(): return lax.fori_loop(0, present, visit, blanks)  15.6 us
  transfers between devices with their start and end apart: 9, of which 7 were waited for; matrix products, arithmetic and copies ran while one was open for 5% of the time, Pallas kernels for 0%

profile of v1, /device:TPU:0, one launch (start us, length us, event | category | flops | bytes accessed | tf_op | source)
XLA Modules:
  0.0 609.9 jit_solution(17946104404329501114)
XLA Ops:
  7.2 0.6 copy-done.2
  7.9 0.7 gather_fusion
  8.6 0.7 gather_fusion.1
  9.3 0.7 gather_fusion.2
  10.0 0.7 gather_fusion.3
  10.7 0.7 dynamic-slice.2
  11.5 11.7 %custom-call.20 = f32[1,128,128]{2,1,0:T(8,128)S(1)} custom-call(f32[1,128,128]{2,1,0:T(8,128)S(1)} %fusion.50), custom_call_target="Cholesky" | custom-call | tf_op jit(solution)/shard_map/jit(cholesky)/cholesky | solution.py:109
  23.2 0.6 compare_reduce_fusion.4
  23.9 0.6 fusion.69
  24.5 9.8 %custom-call.21 = f32[1,1,128,128]{2,3,1,0:T(8,128)S(1)} custom-call(f32[1,1,128,128]{3,2,1,0:T(8,128)S(1)} %fusion.69), custom_call_target="InvertDiagBlocksLowerTriangular" | custom-call | tf_op jit(solution)/shard_map/vmap(jit(_solve_triangular))/triangular_solve | solution.py:32
  35.4 2.2 all-gather
  37.6 1.2 sort.45
  38.9 0.6 broadcast_select_fusion.2
  39.7 0.6 dynamic-slice.3
  40.5 0.7 fusion.114
  41.3 0.7 fusion.112
  42.0 55.4 %all-gather.8.cloned.1.call-done = bf16[32,128,128]{2,1,0:T(8,128)(2,1)} async-done(((bf16[2,128,128]{2,1,0:T(8,128)(2,1)}), bf16[32,128,128]{2,1,0:T(8,128)(2,1)}) %all-gather.8.cloned.1.call-update) | async-done | bytes 1048592 | tf_op jit(solution)/shard_map/while/body/eval_jaxpr/all_gather | solution.py:7
  97.4 1.4 reduce_sum.60
  100.0 11.7 %custom-call.22 = f32[1,128,128]{2,1,0:T(8,128)S(1)} custom-call(f32[1,128,128]{2,1,0:T(8,128)S(1)} %fusion.48), custom_call_target="Cholesky" | custom-call | tf_op jit(solution)/shard_map/jit(cholesky)/cholesky | solution.py:109
  111.7 0.7 compare_reduce_fusion.3
  112.4 0.6 fusion.70
  113.1 9.8 %custom-call.23 = f32[1,1,128,128]{2,3,1,0:T(8,128)S(1)} custom-call(f32[1,1,128,128]{3,2,1,0:T(8,128)S(1)} %fusion.70), custom_call_target="InvertDiagBlocksLowerTriangular" | custom-call | tf_op jit(solution)/shard_map/vmap(jit(_solve_triangular))/triangular_solve | solution.py:32
  123.3 41.5 %all_gather.46 = bf16[16,128,128]{2,1,0:T(8,128)(2,1)S(1)} all-gather(bf16[1,128,128]{2,1,0:T(8,128)(2,1)S(1)} %copy.91), channel_id=1, replica_groups=mesh['col'=16,'grp'=2] {'col'}, dimensions={0}, use_global_device_ids=true | all-gather | bytes 557056 | tf_op jit(solution)/shard_map/all_gather | solution.py:122
  166.1 1.2 sort.46
  167.4 1.2 sort.47
  169.2 11.7 %custom-call.24 = f32[1,128,128]{2,1,0:T(8,128)S(1)} custom-call(f32[1,128,128]{2,1,0:T(8,128)S(1)} %fusion.45), custom_call_target="Cholesky" | custom-call | tf_op jit(solution)/shard_map/jit(cholesky)/cholesky | solution.py:109
  180.9 0.7 compare_reduce_fusion.2
  181.6 0.6 fusion.71
  182.2 9.8 %custom-call.25 = f32[1,1,128,128]{2,3,1,0:T(8,128)S(1)} custom-call(f32[1,1,128,128]{3,2,1,0:T(8,128)S(1)} %fusion.71), custom_call_target="InvertDiagBlocksLowerTriangular" | custom-call | tf_op jit(solution)/shard_map/vmap(jit(_solve_triangular))/triangular_solve | solution.py:32
  192.7 2.1 all-gather.1
  194.8 235.4 %while.48 = (s32[]{:T(128)}, f32[1,2,128,128]{3,2,1,0:T(8,128)S(1)}, f32[1,4,128,128]{3,2,1,0:T(8,128)S(1)}, f32[1,2,128,128]{3,2,1,0:T(8,128)S(1)}, s32[16]{0:T...) while((s32[]{:T(128)}, ...), condition=%wide.region_11.14_spmd.clone, body=%wide.region_9.13_spmd.clone.sunk | while | flops 950288 | bytes 6291798 | solution.py:86
  194.8 0.7 dynamic_slice.120
  196.1 0.6 broadcast_select_fusion.5
  198.7 51.3 %all-gather.10.cloned.1.call-done = bf16[16,2,128,128]{3,2,1,0:T(8,128)(2,1)} async-done(((bf16[1,2,128,128]{3,2,1,0:T(8,128)(2,1)}), bf16[16,2,128,128]{3,2,1,0:T(8,128)(2,1)}) %all-gather.10.cloned.1.call-update) | async-done | bytes 1048592 | tf_op jit(solution)/shard_map/while/body/eval_jaxpr/all_gather | solution.py:7
  250.0 1.4 reduce_sum.68
  251.6 0.7 dynamic_slice.120
  252.9 0.6 broadcast_select_fusion.5
  255.5 54.2 %all-gather.10.cloned.1.call-done = bf16[16,2,128,128]{3,2,1,0:T(8,128)(2,1)} async-done(((bf16[1,2,128,128]{3,2,1,0:T(8,128)(2,1)}), bf16[16,2,128,128]{3,2,1,0:T(8,128)(2,1)}) %all-gather.10.cloned.1.call-update) | async-done | bytes 1048592 | tf_op jit(solution)/shard_map/while/body/eval_jaxpr/all_gather | solution.py:7
  309.7 1.4 reduce_sum.68
  311.4 0.7 dynamic_slice.120
  312.6 0.6 broadcast_select_fusion.5
  315.2 53.9 %all-gather.10.cloned.1.call-done = bf16[16,2,128,128]{3,2,1,0:T(8,128)(2,1)} async-done(((bf16[1,2,128,128]{3,2,1,0:T(8,128)(2,1)}), bf16[16,2,128,128]{3,2,1,0:T(8,128)(2,1)}) %all-gather.10.cloned.1.call-update) | async-done | bytes 1048592 | tf_op jit(solution)/shard_map/while/body/eval_jaxpr/all_gather | solution.py:7
  369.1 1.4 reduce_sum.68
  370.8 0.7 dynamic_slice.120
  372.1 0.6 broadcast_select_fusion.5
  374.6 53.9 %all-gather.10.cloned.1.call-done = bf16[16,2,128,128]{3,2,1,0:T(8,128)(2,1)} async-done(((bf16[1,2,128,128]{3,2,1,0:T(8,128)(2,1)}), bf16[16,2,128,128]{3,2,1,0:T(8,128)(2,1)}) %all-gather.10.cloned.1.call-update) | async-done | bytes 1048592 | tf_op jit(solution)/shard_map/while/body/eval_jaxpr/all_gather | solution.py:7
  428.5 1.4 reduce_sum.68
  430.6 11.7 %custom-call.26 = f32[1,128,128]{2,1,0:T(8,128)S(1)} custom-call(f32[1,128,128]{2,1,0:T(8,128)S(1)} %fusion.41), custom_call_target="Cholesky" | custom-call | tf_op jit(solution)/shard_map/jit(cholesky)/cholesky | solution.py:109
  442.4 0.7 compare_reduce_fusion.1
  443.1 0.6 fusion.72
  443.7 9.8 %custom-call.27 = f32[1,1,128,128]{2,3,1,0:T(8,128)S(1)} custom-call(f32[1,1,128,128]{3,2,1,0:T(8,128)S(1)} %fusion.72), custom_call_target="InvertDiagBlocksLowerTriangular" | custom-call | tf_op jit(solution)/shard_map/vmap(jit(_solve_triangular))/triangular_solve | solution.py:32
  454.1 2.2 all-gather.2
  456.3 119.1 %while.49 = (s32[]{:T(128)}, f32[1,2,128,128]{3,2,1,0:T(8,128)S(1)}, f32[1,4,128,128]{3,2,1,0:T(8,128)S(1)}, f32[1,2,128,128]{3,2,1,0:T(8,128)S(1)}, s32[16]{0:T...) while((s32[]{:T(128)}, ...), condition=%wide.region_15.18_spmd.clone, body=%wide.region_13.17_spmd.clone.sunk | while | flops 950288 | bytes 6291798 | solution.py:86
  457.6 0.6 broadcast_select_fusion.6
  460.2 53.9 %all-gather.12.cloned.1.call-done = bf16[16,2,128,128]{3,2,1,0:T(8,128)(2,1)} async-done(((bf16[1,2,128,128]{3,2,1,0:T(8,128)(2,1)}), bf16[16,2,128,128]{3,2,1,0:T(8,128)(2,1)}) %all-gather.12.cloned.1.call-update) | async-done | bytes 1048592 | tf_op jit(solution)/shard_map/while/body/eval_jaxpr/all_gather | solution.py:7
  514.1 1.4 reduce_sum.69
  517.0 0.6 broadcast_select_fusion.6
  519.6 54.2 %all-gather.12.cloned.1.call-done = bf16[16,2,128,128]{3,2,1,0:T(8,128)(2,1)} async-done(((bf16[1,2,128,128]{3,2,1,0:T(8,128)(2,1)}), bf16[16,2,128,128]{3,2,1,0:T(8,128)(2,1)}) %all-gather.12.cloned.1.call-update) | async-done | bytes 1048592 | tf_op jit(solution)/shard_map/while/body/eval_jaxpr/all_gather | solution.py:7
  573.8 1.4 reduce_sum.69
  575.9 11.7 %custom-call.28 = f32[1,128,128]{2,1,0:T(8,128)S(1)} custom-call(f32[1,128,128]{2,1,0:T(8,128)S(1)} %fusion.36), custom_call_target="Cholesky" | custom-call | tf_op jit(solution)/shard_map/jit(cholesky)/cholesky | solution.py:109
  587.7 0.6 compare_reduce_fusion
  588.3 3.7 select_bitcast_fusion
  592.0 9.8 %custom-call.29 = f32[1,1,128,128]{2,3,1,0:T(8,128)S(1)} custom-call(f32[1,1,128,128]{3,2,1,0:T(8,128)S(1)} %get-tuple-element.607), custom_call_target="InvertDiagBlocksLowerTriangular" | custom-call | tf_op jit(solution)/shard_map/vmap(jit(_solve_triangular))/triangular_solve | solution.py:32
  602.3 0.7 copy.109
  (134 shorter events, 10.1 us)
Async XLA Ops:
  7.2 0.7 copy-start.2
  7.2 90.2 %all-gather.8.cloned.1.call-start = ((), (), s32[]{:S(2)}) async-start(), calls=%async_computation | async-start | bytes 1114112 | tf_op jit(solution)/shard_map/while/body/eval_jaxpr/all_gather | solution.py:7
  10.0 1.4 copy-start
  23.9 11.1 %copy-start.1 = (f32[1,1,128,128]{3,2,1,0:T(8,128)S(1)}, f32[1,1,128,128]{3,2,1,0:T(8,128)}, u32[]{:S(2)}) copy-start(f32[1,1,128,128]{3,2,1,0:T(8,128)} %param.14) | copy-start | bytes 196612
  166.0 3.1 collective-permute-start
  168.6 23.4 %collective-permute-start.1 = (bf16[1,2,128,128]{3,1,2,0:T(2,128)(2,1)S(1)}, bf16[1,2,128,128]{3,1,2,0:T(2,128)(2,1)S(1)}, u32[]{:S(2)}, u32[]{:S(2)}) collective-permute-start(bf16[1,2,128,128]{3,1,2,0:T(2,128)(2,1)S(1)} %bitcast.316), channel_id=1, source_target_pairs={{0,1},{1,0},{2,3},{3,2},{4,5},{5,4},{6,7},{7,6},{8,9},{9,8},{10,11... | collective-permute-start | bytes 196616 | tf_op jit(solution)/shard_map/ppermute | solution.py:16
  194.8 55.2 %all-gather.10.cloned.1.call-start = ((), (), s32[]{:S(2)}) async-start(), calls=%async_computation.1 | async-start | bytes 1114112 | tf_op jit(solution)/shard_map/while/body/eval_jaxpr/all_gather | solution.py:7
  251.6 58.1 %all-gather.10.cloned.1.call-start = ((), (), s32[]{:S(2)}) async-start(), calls=%async_computation.1 | async-start | bytes 1114112 | tf_op jit(solution)/shard_map/while/body/eval_jaxpr/all_gather | solution.py:7
  311.3 57.8 %all-gather.10.cloned.1.call-start = ((), (), s32[]{:S(2)}) async-start(), calls=%async_computation.1 | async-start | bytes 1114112 | tf_op jit(solution)/shard_map/while/body/eval_jaxpr/all_gather | solution.py:7
  370.7 57.8 %all-gather.10.cloned.1.call-start = ((), (), s32[]{:S(2)}) async-start(), calls=%async_computation.1 | async-start | bytes 1114112 | tf_op jit(solution)/shard_map/while/body/eval_jaxpr/all_gather | solution.py:7
  456.3 57.8 %all-gather.12.cloned.1.call-start = ((), (), s32[]{:S(2)}) async-start(), calls=%async_computation.2 | async-start | bytes 1114112 | tf_op jit(solution)/shard_map/while/body/eval_jaxpr/all_gather | solution.py:7
  515.7 58.1 %all-gather.12.cloned.1.call-start = ((), (), s32[]{:S(2)}) async-start(), calls=%async_computation.2 | async-start | bytes 1114112 | tf_op jit(solution)/shard_map/while/body/eval_jaxpr/all_gather | solution.py:7
Sparse Core Ops, SparseCore 0:
  39.7 57.6 all-gather.7
  198.9 50.9 all-gather.9
  255.7 53.9 all-gather.9
  315.2 53.9 all-gather.9
  374.6 53.9 all-gather.9
  460.1 53.9 all-gather.11
  519.8 53.9 all-gather.11
